TPU v7x, 256 devices: a whole 4x4x8 slice. The times are simulated.
256 devices in a mesh: zonal: 64 (over y_lo, x, z), merid: 4 (over y_hi, core).
Axes of the slice: x: 4, y: 4 (y_hi: 2, y_lo: 2; y = y_hi * 2 + y_lo), z: 8, core: 2. Of those that a mesh axis runs over, the one named last changes fastest.
Arguments:
- field: bfloat16 [64, 4096, 256], P('merid', 'zonal'), may hold values from -6 to 6
- weight_one: bfloat16 [3, 3, 256, 256], replicated, may hold values from -0.125 to 0.125
- bias_one: float32 [256], replicated, may hold values from -3 to 3
- weight_two: bfloat16 [3, 3, 256, 256], replicated, may hold values from -0.125 to 0.125
- bias_two: float32 [256], replicated, may hold values from -3 to 3
- depth_levels: int32 [64, 4096], P('merid', 'zonal'), may hold values from 0 to 64
- fold_partner: int32 [4096], replicated, may hold values from 0 to 4095, as said below
- cotangent: bfloat16 [64, 4096, 256], P('merid', 'zonal'), may hold values from -6 to 6
Outputs:
- output: bfloat16 [64, 4096, 256], P('merid', 'zonal')
- input_grad: bfloat16 [64, 4096, 256], P('merid', 'zonal')
- grad_one: float32 [3, 3, 256, 256], replicated
- grad_two: float32 [3, 3, 256, 256], replicated
Inputs may be any that keep to these rules, and one draw needn't show every extreme that they name: fold_partner[i] = (4095 - i + s) mod 4096 with one pivot offset s, 0 to 4095, for the whole table.
All inputs are finite; a program needn't handle non-finite values.
Results may differ from a plain program's by a relative error of at most 0.003.
Values may be sent and summed in bfloat16 or wider, within the bound.
No kernel may reach another device: no remote copies, remote signals or barrier semaphores. Data moves between devices by JAX's collectives and lax.ppermute only.
A program may use at most 128 MiB of HBM per device.

v0:
```python
import math
import jax
import jax.numpy as jnp
from jax import lax
from jax.sharding import PartitionSpec as P

LEV = 64


def with_halo(cells, sides, width, closed):
    for axis, dim in sides:
        count = lax.axis_size(axis)
        ends = count if closed else count - 1
        head = lax.slice_in_dim(cells, 0, width, axis=dim)
        tail = lax.slice_in_dim(cells, cells.shape[dim] - width, cells.shape[dim], axis=dim)
        cells = jnp.concatenate(
            [
                lax.ppermute(tail, axis, [(i, (i + 1) % count) for i in range(ends)]),
                cells,
                lax.ppermute(head, axis, [((i + 1) % count, i) for i in range(ends)]),
            ],
            axis=dim,
        )
    return cells


def level_mask(depth_levels, channels):
    level_index = lax.broadcasted_iota(jnp.int32, (1, 1, channels), 2) % LEV
    return (level_index < depth_levels[:, :, None]).astype(jnp.float32)


def fold_forward(top_row, fold_partner):
    columns = top_row.shape[0]
    whole_row = lax.all_gather(top_row, "zonal", axis=0, tiled=True)
    partners = lax.dynamic_slice_in_dim(fold_partner, lax.axis_index("zonal") * columns, columns, 0)
    return jnp.take(whole_row, partners, axis=0)


def fold_backward(fold_grad, fold_partner):
    columns = fold_grad.shape[0]
    whole_row = lax.all_gather(fold_grad.astype(jnp.bfloat16), "zonal", axis=0, tiled=True).astype(
        fold_grad.dtype
    )
    partners = lax.dynamic_slice_in_dim(fold_partner, lax.axis_index("zonal") * columns, columns, 0)
    return jnp.take(whole_row, partners, axis=0)


def pad_field(values, fold_partner, is_top):
    with_rows = with_halo(values, (("merid", 0),), 1, False)
    fold_row = fold_forward(values[-1], fold_partner)
    upper_row = jnp.where(is_top, fold_row, with_rows[-1])
    with_rows = jnp.concatenate([with_rows[:-1], upper_row[None]], axis=0)
    return with_halo(with_rows, (("zonal", 1),), 1, True)


def unpad_grad(grad_pad, fold_partner, is_top):
    sides = jnp.concatenate([grad_pad[:, :1], grad_pad[:, -1:]], axis=1)
    returned = with_halo(sides.astype(jnp.bfloat16), (("zonal", 1),), 1, True).astype(sides.dtype)
    inner = grad_pad[:, 1:-1]
    inner = inner.at[:, 0].add(returned[:, 0]).at[:, -1].add(returned[:, 3])
    rims = jnp.concatenate([inner[:1], inner[-1:]], axis=0)
    back_rows = with_halo(rims.astype(jnp.bfloat16), (("merid", 0),), 1, False).astype(rims.dtype)
    folded = fold_backward(inner[-1], fold_partner)
    top_added = back_rows[3] + jnp.where(is_top, folded, jnp.zeros_like(folded))
    middle = inner[1:-1]
    return middle.at[0].add(back_rows[0]).at[-1].add(top_added)


def patches_of(padded, rows, columns):
    pieces = [
        padded[row_step : row_step + rows, col_step : col_step + columns]
        for row_step in range(3)
        for col_step in range(3)
    ]
    return jnp.concatenate(pieces, axis=2).reshape(rows * columns, -1)


def transpose_conv(delta, flat_weight, rows, columns):
    channels = delta.shape[1]
    parts = lax.dot_general(
        delta, flat_weight, (((1,), (1,)), ((), ())), preferred_element_type=jnp.float32
    )
    parts = parts.reshape(rows, columns, 9, channels)
    grad_pad = jnp.zeros((rows + 2, columns + 2, channels), jnp.float32)
    for row_step in range(3):
        for col_step in range(3):
            grad_pad = grad_pad.at[row_step : row_step + rows, col_step : col_step + columns].add(
                parts[:, :, 3 * row_step + col_step]
            )
    return grad_pad


def kernel_grad(patches, delta):
    channels = delta.shape[1]
    summed = lax.dot_general(
        patches, delta, (((0,), (0,)), ((), ())), preferred_element_type=jnp.float32
    )
    return summed.reshape(3, 3, channels, channels)


def shards(
    field, weight_one, bias_one, weight_two, bias_two, depth_levels, fold_partner, cotangent
):
    rows, columns, channels = field.shape
    is_top = lax.axis_index("merid") == lax.axis_size("merid") - 1
    mask = level_mask(depth_levels, channels)
    flat_one = weight_one.reshape(9 * channels, channels)
    flat_two = weight_two.reshape(9 * channels, channels)
    patches_one = patches_of(pad_field(field, fold_partner, is_top), rows, columns)
    pre_one = (
        jnp.dot(patches_one, flat_one, preferred_element_type=jnp.float32).reshape(
            rows, columns, channels
        )
        + bias_one
    )
    hidden = (jax.nn.gelu(pre_one) * mask).astype(jnp.bfloat16)
    patches_two = patches_of(pad_field(hidden, fold_partner, is_top), rows, columns)
    pre_two = jnp.dot(patches_two, flat_two, preferred_element_type=jnp.float32).reshape(
        rows, columns, channels
    )
    output = ((field.astype(jnp.float32) + pre_two + bias_two) * mask).astype(jnp.bfloat16)
    masked_grad = cotangent.astype(jnp.float32) * mask
    delta_two = masked_grad.astype(jnp.bfloat16).reshape(rows * columns, channels)
    grad_two = kernel_grad(patches_two, delta_two)
    hidden_grad = unpad_grad(
        transpose_conv(delta_two, flat_two, rows, columns), fold_partner, is_top
    )
    _, gelu_back = jax.vjp(jax.nn.gelu, pre_one)
    delta_one = (
        gelu_back(hidden_grad * mask)[0].astype(jnp.bfloat16).reshape(rows * columns, channels)
    )
    grad_one = kernel_grad(patches_one, delta_one)
    field_grad = unpad_grad(
        transpose_conv(delta_one, flat_one, rows, columns), fold_partner, is_top
    )
    input_grad = (masked_grad + field_grad).astype(jnp.bfloat16)
    grad_one, grad_two = lax.psum((grad_one, grad_two), ("zonal", "merid"))
    scale = 1.0 / math.sqrt(rows * columns * lax.axis_size("zonal") * lax.axis_size("merid"))
    return (output, input_grad, grad_one * scale, grad_two * scale)


def solution(mesh):
    placed = (
        P("merid", "zonal", None),
        P(),
        P(),
        P(),
        P(),
        P("merid", "zonal"),
        P(),
        P("merid", "zonal", None),
    )
    return jax.shard_map(
        shards,
        mesh=mesh,
        in_specs=placed,
        out_specs=(P("merid", "zonal", None), P("merid", "zonal", None), P(), P()),
        check_vma=False,
    )
```

profile of v0, /device:TPU:97, one launch (start us, length us, event | category | flops | bytes accessed | tf_op | source)
XLA Modules:
  0.0 1509.0 jit_solution(12286972379343277605)
XLA Ops:
  19.0 6.4 scatter-add.89
  31.1 6.4 scatter-add.90
  41.3 5.1 scatter-add.94
  48.8 5.1 scatter-add.95
  57.8 5.1 scatter-add.99
  65.3 5.1 scatter-add.100
  83.2 6.8 collective-permute-start
  94.1 5.1 collective-permute-start.10
  101.2 157.8 %all-gather.9.cloned.1.call-done = bf16[1,4096,256]{2,1,0:T(8,128)(2,1)} async-done(((bf16[1,64,256]{2,1,0:T(8,128)(2,1)}), bf16[1,4096,256]{2,1,0:T(8,128)(2,1)}) %all-gather.9.cloned.1.call-update) | async-done | bytes 2097168 | tf_op jit(solution)/shard_map/all_gather | solution.py:34
  276.2 282.4 %all-gather.13.cloned.1.call-done = bf16[1,4096,256]{2,1,0:T(8,128)(2,1)} async-done(((bf16[1,64,256]{2,1,0:T(8,128)(2,1)}), bf16[1,4096,256]{2,1,0:T(8,128)(2,1)}) %all-gather.13.cloned.1.call-update) | async-done | bytes 2097168 | tf_op jit(solution)/shard_map/all_gather | solution.py:41
  565.4 5.2 fusion.8
  579.7 6.4 scatter-add.110
  619.2 50.8 %collective-permute-start.5 = (bf16[1,64,256]{2,1,0:T(8,128)(2,1)}, bf16[1,64,256]{2,1,0:T(8,128)(2,1)S(1)}, u32[]{:S(2)}, u32[]{:S(2)}) collective-permute-start(bf16[1,64,256]{2,1,0:T(8,128)(2,1)} %get-tuple-element.341), channel_id=1, source_target_pairs={{1,0},{2,1},{3,2},{5,4},{6,5},{7,6},{9,8},{10,9},{11,10},{13,12},{... | collective-permute-start | bytes 98312 | tf_op jit(solution)/shard_map/ppermute | solution.py:20
  674.3 6.8 copy.30
  681.1 187.6 %all-gather.11.cloned.1.call-done = bf16[1,4096,256]{2,1,0:T(8,128)(2,1)} async-done(((bf16[1,64,256]{2,1,0:T(8,128)(2,1)}), bf16[1,4096,256]{2,1,0:T(8,128)(2,1)}) %all-gather.11.cloned.1.call-update) | async-done | bytes 2097168 | tf_op jit(solution)/shard_map/all_gather | solution.py:34
  876.0 5.1 fusion.55
  884.6 6.8 copy.31
  891.4 5.1 fusion.56
  897.3 52.6 %collective-permute-start.14 = (bf16[1,64,256]{2,1,0:T(8,128)(2,1)S(1)}, bf16[1,64,256]{2,1,0:T(8,128)(2,1)S(1)}, u32[]{:S(2)}, u32[]{:S(2)}) collective-permute-start(bf16[1,64,256]{2,1,0:T(8,128)(2,1)S(1)} %copy-done.14), channel_id=1, source_target_pairs={{0,1},{1,2},{2,3},{4,5},{5,6},{6,7},{8,9},{9,10},{10,11},{12,13},{... | collective-permute-start | bytes 98312 | tf_op jit(solution)/shard_map/ppermute | solution.py:18
  951.9 4.7 collective-permute-done.15
  956.7 211.5 %all-gather.15.cloned.1.call-done = bf16[1,4096,256]{2,1,0:T(8,128)(2,1)} async-done(((bf16[1,64,256]{2,1,0:T(8,128)(2,1)}), bf16[1,4096,256]{2,1,0:T(8,128)(2,1)}) %all-gather.15.cloned.1.call-update) | async-done | bytes 2097168 | tf_op jit(solution)/shard_map/all_gather | solution.py:41
  1176.3 4.5 fusion.1
  1180.8 316.5 %all-reduce.5.cloned.1.call-done = (f32[3,3,256,256]{3,2,1,0:T(8,128)}, f32[3,3,256,256]{3,2,1,0:T(8,128)}) async-done(((f32[3,3,256,256]{3,2,1,0:T(8,128)}, f32[3,3,256,256]{3,2,1,0:T(8,128)}), (f32[3,3,256,256]{3,2,1,0:T(8,128)}, f32[3,3,256,256]{3,2,1,0:T(8,128)})) %all-reduce.5.cloned.1.call-update) | async-done | bytes 4718608 | tf_op jit(solution)/shard_map/psum | solution.py:137
  1497.3 5.1 broadcast_multiply_fusion
  (188 shorter events, 140.1 us)
Async XLA Ops:
  7.2 558.2 %copy-start = (bf16[3,3,256,256]{3,2,1,0:T(8,128)(2,1)S(1)}, bf16[3,3,256,256]{3,2,1,0:T(8,128)(2,1)}, u32[]{:S(2)}) copy-start(bf16[3,3,256,256]{3,2,1,0:T(8,128)(2,1)} %param.65) | copy-start | bytes 3538948
  7.2 251.8 %all-gather.9.cloned.1.call-start = ((), (), s32[]{:S(2)}) async-start(), calls=%async_computation | async-start | bytes 2129920 | tf_op jit(solution)/shard_map/all_gather | solution.py:34
  8.7 549.8 %all-gather.13.cloned.1.call-start = ((), (), s32[]{:S(2)}) async-start(), calls=%async_computation.2 | async-start | bytes 2129920 | tf_op jit(solution)/shard_map/all_gather | solution.py:41
  8.8 556.6 %copy-start.25 = (s32[256]{0:T(256)}, s32[256]{0:T(256)S(1)}, u32[]{:S(2)}) copy-start(s32[256]{0:T(256)S(1)} %and_select_fusion) | copy-start | bytes 3076
  70.5 4.1 collective-permute-start.8
  73.4 3.8 collective-permute-start.9
  83.2 785.5 %all-gather.11.cloned.1.call-start = ((), (), s32[]{:S(2)}) async-start(), calls=%async_computation.1 | async-start | bytes 2129920 | tf_op jit(solution)/shard_map/all_gather | solution.py:34
  83.2 178.4 %collective-permute-start = (bf16[1,64,256]{2,1,0:T(8,128)(2,1)S(1)}, bf16[1,64,256]{2,1,0:T(8,128)(2,1)S(1)}, u32[]{:S(2)}, u32[]{:S(2)}) collective-permute-start(bf16[1,64,256]{2,1,0:T(8,128)(2,1)S(1)} %copy-done.17), channel_id=1, source_target_pairs={{0,1},{1,2},{2,3},{4,5},{5,6},{6,7},{8,9},{9,10},{10,11},{12,13},{... | collective-permute-start | bytes 98312 | tf_op jit(solution)/shard_map/ppermute | solution.py:18
  90.1 171.5 %collective-permute-start.1 = (bf16[1,64,256]{2,1,0:T(8,128)(2,1)S(1)}, bf16[1,64,256]{2,1,0:T(8,128)(2,1)S(1)}, u32[]{:S(2)}, u32[]{:S(2)}) collective-permute-start(bf16[1,64,256]{2,1,0:T(8,128)(2,1)S(1)} %get-tuple-element.343), channel_id=1, source_target_pairs={{1,0},{2,1},{3,2},{5,4},{6,5},{7,6},{9,8},{10,9},{11,10},{13,12},{... | collective-permute-start | bytes 98312 | tf_op jit(solution)/shard_map/ppermute | solution.py:20
  92.8 472.5 %copy-start.22 = (pred[64]{0:T(512)(128)(4,1)}, pred[64]{0:T(512)(128)(4,1)S(1)}, u32[]{:S(2)}) copy-start(pred[64]{0:T(512)(128)(4,1)S(1)} %get-tuple-element.320) | copy-start | bytes 196
  94.1 172.1 %collective-permute-start.10 = (bf16[1,64,256]{2,1,0:T(8,128)(2,1)}, bf16[1,64,256]{2,1,0:T(8,128)(2,1)S(1)}, u32[]{:S(2)}, u32[]{:S(2)}) collective-permute-start(bf16[1,64,256]{2,1,0:T(8,128)(2,1)} %get-tuple-element.324), channel_id=1, source_target_pairs={{0,1},{1,2},{2,3},{4,5},{5,6},{6,7},{8,9},{9,10},{10,11},{12,13},{... | collective-permute-start | bytes 98312 | tf_op jit(solution)/shard_map/ppermute | solution.py:18
  99.3 167.0 %collective-permute-start.11 = (bf16[1,64,256]{2,1,0:T(8,128)(2,1)S(1)}, bf16[1,64,256]{2,1,0:T(8,128)(2,1)S(1)}, u32[]{:S(2)}, u32[]{:S(2)}) collective-permute-start(bf16[1,64,256]{2,1,0:T(8,128)(2,1)S(1)} %get-tuple-element.325), channel_id=1, source_target_pairs={{1,0},{2,1},{3,2},{5,4},{6,5},{7,6},{9,8},{10,9},{11,10},{13,12},{... | collective-permute-start | bytes 98312 | tf_op jit(solution)/shard_map/ppermute | solution.py:20
  261.7 5.7 collective-permute-start.2
  262.9 4.4 collective-permute-start.3
  571.2 596.9 %all-gather.15.cloned.1.call-start = ((), (), s32[]{:S(2)}) async-start(), calls=%async_computation.3 | async-start | bytes 2129920 | tf_op jit(solution)/shard_map/all_gather | solution.py:41
  609.3 5.5 collective-permute-start.12
  610.6 4.2 collective-permute-start.13
  619.1 878.2 %all-reduce.5.cloned.1.call-start = ((), (), s32[]{:S(2)}) async-start(), calls=%async_computation.4 | async-start | bytes 9437184 | tf_op jit(solution)/shard_map/psum | solution.py:137
  619.2 252.2 %collective-permute-start.5 = (bf16[1,64,256]{2,1,0:T(8,128)(2,1)}, bf16[1,64,256]{2,1,0:T(8,128)(2,1)S(1)}, u32[]{:S(2)}, u32[]{:S(2)}) collective-permute-start(bf16[1,64,256]{2,1,0:T(8,128)(2,1)} %get-tuple-element.341), channel_id=1, source_target_pairs={{1,0},{2,1},{3,2},{5,4},{6,5},{7,6},{9,8},{10,9},{11,10},{13,12},{... | collective-permute-start | bytes 98312 | tf_op jit(solution)/shard_map/ppermute | solution.py:20
  670.0 201.4 %collective-permute-start.4 = (bf16[1,64,256]{2,1,0:T(8,128)(2,1)}, bf16[1,64,256]{2,1,0:T(8,128)(2,1)S(1)}, u32[]{:S(2)}, u32[]{:S(2)}) collective-permute-start(bf16[1,64,256]{2,1,0:T(8,128)(2,1)} %get-tuple-element.340), channel_id=1, source_target_pairs={{0,1},{1,2},{2,3},{4,5},{5,6},{6,7},{8,9},{9,10},{10,11},{12,13},{... | collective-permute-start | bytes 98312 | tf_op jit(solution)/shard_map/ppermute | solution.py:18
  871.5 9.7 collective-permute-start.6
  873.5 7.7 collective-permute-start.7
  897.3 54.6 %collective-permute-start.14 = (bf16[1,64,256]{2,1,0:T(8,128)(2,1)S(1)}, bf16[1,64,256]{2,1,0:T(8,128)(2,1)S(1)}, u32[]{:S(2)}, u32[]{:S(2)}) collective-permute-start(bf16[1,64,256]{2,1,0:T(8,128)(2,1)S(1)} %copy-done.14), channel_id=1, source_target_pairs={{0,1},{1,2},{2,3},{4,5},{5,6},{6,7},{8,9},{9,10},{10,11},{12,13},{... | collective-permute-start | bytes 98312 | tf_op jit(solution)/shard_map/ppermute | solution.py:18
  949.9 6.7 collective-permute-start.15
  (27 other events, 2656.5 us)
Sparse Core Ops, SparseCore 0:
  10.4 248.6 all-gather.8
  261.4 297.1 all-gather.12
  571.4 297.2 all-gather.10
  870.3 297.7 all-gather.14
  1174.2 323.0 all-reduce.4
where the time goes:
time: 1510 us
  waiting for transfers between devices  1160 us (77%)
  starting transfers between devices  142 us (9%)
  local copies, waits for them, and re-layouts  106 us (7%)
  other arithmetic  56.4 us (4%)
  matrix products  25.3 us (2%)
    all_gather x2, waiting for transfers between devices, fold_backward(): lax.all_gather(fold_grad.astype(jnp.bfloat16), 'zonal', axis=0, tiled=True)  494 us
    all_gather x2, waiting for transfers between devices, fold_forward(): whole_row = lax.all_gather(top_row, 'zonal', axis=0, tiled=True)  345 us
    psum x1, waiting for transfers between devices, shards(): grad_one, grad_two = lax.psum((grad_one, grad_two), ('zonal', 'merid'))  317 us
    ppermute x8, starting transfers between devices, with_halo(): lax.ppermute(tail, axis, [(i, (i + 1) % count) for i in range(ends)])  76.3 us
    ppermute x8, starting transfers between devices, with_halo(): lax.ppermute(head, axis, [((i + 1) % count, i) for i in range(ends)])  65.5 us
    scatter-add x14, local copies, waits for them, and re-layouts, transpose_conv(): grad_pad.at[row_step:row_step + rows, col_step:col_step + columns]  51.2 us
  transfers between devices with their start and end apart: 21, of which 9 were waited for; matrix products, arithmetic and copies ran while one was open for 10% of the time, Pallas kernels for 0%

commit v1 on v0

--- a/solution.py
+++ b/solution.py
@@ -1,3 +1,4 @@
+import functools
 import math
 import jax
 import jax.numpy as jnp
@@ -5,6 +6,22 @@
 from jax.sharding import PartitionSpec as P
 
 LEV = 64
+
+
+def draft_object(my_tile, mesh_ax, at_axis):
+    m_next = jnp.concatenate(
+        lax.all_to_all(
+            jnp.stack([my_tile] * lax.axis_size(mesh_ax)),
+            axis_name=mesh_ax,
+            split_axis=0,
+            concat_axis=0,
+        ),
+        axis=at_axis,
+    )
+    return m_next
+
+
+_obtain_slabs = functools.partial(draft_object, mesh_ax="zonal", at_axis=0)
 
 
 def with_halo(cells, sides, width, closed):
@@ -31,7 +48,7 @@
 
 def fold_forward(top_row, fold_partner):
     columns = top_row.shape[0]
-    whole_row = lax.all_gather(top_row, "zonal", axis=0, tiled=True)
+    whole_row = _obtain_slabs(top_row)
     partners = lax.dynamic_slice_in_dim(fold_partner, lax.axis_index("zonal") * columns, columns, 0)
     return jnp.take(whole_row, partners, axis=0)
 

time: 1510 us -> 1060 us (0.70)
  waiting for transfers between devices: 1160 us -> 739 us
  starting transfers between devices: 142 us -> 116 us
    all_gather x2 -> x0, waiting for transfers between devices: 345 us -> none  [fold_forward(): whole_row = lax.all_gather(top_row, 'zonal', axis=0, tiled=True)]
    all_gather x2, waiting for transfers between devices: 494 us -> 414 us  [fold_backward(): lax.all_gather(fold_grad.astype(jnp.bfloat16), 'zonal', axis=0, tiled=True)]
    ppermute x8, starting transfers between devices: 76.3 us -> 32.1 us  [with_halo(): lax.ppermute(tail, axis, [(i, (i + 1) % count) for i in range(ends)])]
    all_to_all x0 -> x2, starting transfers between devices: none -> 24.1 us  [draft_object(): lax.all_to_all(jnp.stack([my_tile] * lax.axis_size(mesh_ax)), axis_name=m...]
  transfers between devices with their start and end apart: 21 -> 21, of which waited for: 9 -> 8; matrix products, arithmetic and copies ran while one was open for 10% -> 15% of each run, Pallas kernels for 0% -> 0%
where the time goes in v1:
time: 1060 us
  waiting for transfers between devices  739 us (70%)
  starting transfers between devices  116 us (11%)
  local copies, waits for them, and re-layouts  107 us (10%)
  other arithmetic  55.5 us (5%)
  matrix products  22.8 us (2%)
  between operations  14.6 us (1%)
    all_gather x2, waiting for transfers between devices, fold_backward(): lax.all_gather(fold_grad.astype(jnp.bfloat16), 'zonal', axis=0, tiled=True)  414 us
    psum x1, waiting for transfers between devices, shards(): grad_one, grad_two = lax.psum((grad_one, grad_two), ('zonal', 'merid'))  318 us
    ppermute x8, starting transfers between devices, with_halo(): lax.ppermute(head, axis, [((i + 1) % count, i) for i in range(ends)])  60.2 us
    scatter-add x14, local copies, waits for them, and re-layouts, transpose_conv(): grad_pad.at[row_step:row_step + rows, col_step:col_step + columns]  51.1 us
    ppermute x8, starting transfers between devices, with_halo(): lax.ppermute(tail, axis, [(i, (i + 1) % count) for i in range(ends)])  32.1 us
    all_to_all x2, starting transfers between devices, draft_object(): lax.all_to_all(jnp.stack([my_tile] * lax.axis_size(mesh_ax)), axis_name=m...  24.1 us
  transfers between devices with their start and end apart: 21, of which 8 were waited for; matrix products, arithmetic and copies ran while one was open for 15% of the time, Pallas kernels for 0%

profile of v1, /device:TPU:97, one launch (start us, length us, event | category | flops | bytes accessed | tf_op | source)
XLA Modules:
  0.0 1055.1 jit_solution(16497872787932612438)
XLA Ops:
  9.6 11.5 %all-to-all-start = ((bf16[64,64,256]{2,1,0:T(8,128)(2,1)}), bf16[64,64,256]{2,1,0:T(8,128)(2,1)}, u32[]{:S(2)}, u32[]{:S(2)}) async-start(bf16[64,64,256]{2,1,0:T(8,128)(2,1)} %stack.6), calls=%async_computation | async-start | bytes 4194304 | tf_op jit(solution)/shard_map/all_to_all | solution.py:13
  30.1 6.4 scatter-add.89
  40.7 6.4 scatter-add.90
  50.9 5.1 scatter-add.94
  58.4 5.1 scatter-add.95
  67.3 5.1 scatter-add.99
  74.8 5.1 scatter-add.100
  92.3 7.1 collective-permute-start
  102.1 5.1 collective-permute-start.10
  125.9 215.2 %all-gather.5.cloned.1.call-done = bf16[1,4096,256]{2,1,0:T(8,128)(2,1)} async-done(((bf16[1,64,256]{2,1,0:T(8,128)(2,1)}), bf16[1,4096,256]{2,1,0:T(8,128)(2,1)}) %all-gather.5.cloned.1.call-update) | async-done | bytes 2097168 | tf_op jit(solution)/shard_map/all_gather | solution.py:58
  348.0 5.2 fusion.8
  355.4 12.7 %all-to-all-start.1 = ((bf16[64,64,256]{2,1,0:T(8,128)(2,1)}), bf16[64,64,256]{2,1,0:T(8,128)(2,1)}, u32[]{:S(2)}, u32[]{:S(2)}) async-start(bf16[64,64,256]{2,1,0:T(8,128)(2,1)} %stack.7), calls=%async_computation.1 | async-start | bytes 4194304 | tf_op jit(solution)/shard_map/all_to_all | solution.py:13
  375.5 6.4 scatter-add.110
  415.1 53.9 %collective-permute-start.5 = (bf16[1,64,256]{2,1,0:T(8,128)(2,1)}, bf16[1,64,256]{2,1,0:T(8,128)(2,1)S(1)}, u32[]{:S(2)}, u32[]{:S(2)}) collective-permute-start(bf16[1,64,256]{2,1,0:T(8,128)(2,1)} %get-tuple-element.342), channel_id=1, source_target_pairs={{1,0},{2,1},{3,2},{5,4},{6,5},{7,6},{9,8},{10,9},{11,10},{13,12},{... | collective-permute-start | bytes 98312 | tf_op jit(solution)/shard_map/ppermute | solution.py:37
  469.1 6.8 copy.30
  475.8 4.4 collective-permute-start.4
  486.0 5.1 fusion.55
  494.6 6.8 copy.31
  501.4 5.1 fusion.56
  508.6 5.1 collective-permute-start.14
  514.8 198.4 %all-gather.7.cloned.1.call-done = bf16[1,4096,256]{2,1,0:T(8,128)(2,1)} async-done(((bf16[1,64,256]{2,1,0:T(8,128)(2,1)}), bf16[1,4096,256]{2,1,0:T(8,128)(2,1)}) %all-gather.7.cloned.1.call-update) | async-done | bytes 2097168 | tf_op jit(solution)/shard_map/all_gather | solution.py:58
  721.3 4.5 fusion.1
  725.8 317.7 %all-reduce.5.cloned.1.call-done = (f32[3,3,256,256]{3,2,1,0:T(8,128)}, f32[3,3,256,256]{3,2,1,0:T(8,128)}) async-done(((f32[3,3,256,256]{3,2,1,0:T(8,128)}, f32[3,3,256,256]{3,2,1,0:T(8,128)}), (f32[3,3,256,256]{3,2,1,0:T(8,128)}, f32[3,3,256,256]{3,2,1,0:T(8,128)})) %all-reduce.5.cloned.1.call-update) | async-done | bytes 4718608 | tf_op jit(solution)/shard_map/psum | solution.py:154
  1043.5 5.1 broadcast_multiply_fusion
  (194 shorter events, 131.1 us)
Async XLA Ops:
  7.2 340.8 %copy-start = (bf16[3,3,256,256]{3,2,1,0:T(8,128)(2,1)S(1)}, bf16[3,3,256,256]{3,2,1,0:T(8,128)(2,1)}, u32[]{:S(2)}) copy-start(bf16[3,3,256,256]{3,2,1,0:T(8,128)(2,1)} %param.65) | copy-start | bytes 3538948
  9.6 100.9 %all-to-all-start = ((bf16[64,64,256]{2,1,0:T(8,128)(2,1)}), bf16[64,64,256]{2,1,0:T(8,128)(2,1)}, u32[]{:S(2)}, u32[]{:S(2)}) async-start(bf16[64,64,256]{2,1,0:T(8,128)(2,1)} %stack.6), calls=%async_computation | async-start | bytes 4194304 | tf_op jit(solution)/shard_map/all_to_all | solution.py:13
  21.1 320.0 %all-gather.5.cloned.1.call-start = ((), (), s32[]{:S(2)}) async-start(), calls=%async_computation.2 | async-start | bytes 2129920 | tf_op jit(solution)/shard_map/all_gather | solution.py:58
  21.2 326.8 %copy-start.28 = (s32[256]{0:T(256)}, s32[256]{0:T(256)S(1)}, u32[]{:S(2)}) copy-start(s32[256]{0:T(256)S(1)} %and_select_fusion) | copy-start | bytes 3076
  80.1 3.6 collective-permute-start.8
  82.5 3.8 collective-permute-start.9
  92.3 20.8 %collective-permute-start = (bf16[1,64,256]{2,1,0:T(8,128)(2,1)S(1)}, bf16[1,64,256]{2,1,0:T(8,128)(2,1)S(1)}, u32[]{:S(2)}, u32[]{:S(2)}) collective-permute-start(bf16[1,64,256]{2,1,0:T(8,128)(2,1)S(1)} %get-tuple-element.343), channel_id=1, source_target_pairs={{0,1},{1,2},{2,3},{4,5},{5,6},{6,7},{8,9},{9,10},{10,11},{12,13},{... | collective-permute-start | bytes 98312 | tf_op jit(solution)/shard_map/ppermute | solution.py:35
  99.4 13.7 %collective-permute-start.1 = (bf16[1,64,256]{2,1,0:T(8,128)(2,1)S(1)}, bf16[1,64,256]{2,1,0:T(8,128)(2,1)S(1)}, u32[]{:S(2)}, u32[]{:S(2)}) collective-permute-start(bf16[1,64,256]{2,1,0:T(8,128)(2,1)S(1)} %get-tuple-element.345), channel_id=1, source_target_pairs={{1,0},{2,1},{3,2},{5,4},{6,5},{7,6},{9,8},{10,9},{11,10},{13,12},{... | collective-permute-start | bytes 98312 | tf_op jit(solution)/shard_map/ppermute | solution.py:37
  102.1 245.8 %copy-start.25 = (pred[64]{0:T(512)(128)(4,1)}, pred[64]{0:T(512)(128)(4,1)S(1)}, u32[]{:S(2)}) copy-start(pred[64]{0:T(512)(128)(4,1)S(1)} %get-tuple-element.320) | copy-start | bytes 196
  102.1 13.9 %collective-permute-start.10 = (bf16[1,64,256]{2,1,0:T(8,128)(2,1)}, bf16[1,64,256]{2,1,0:T(8,128)(2,1)S(1)}, u32[]{:S(2)}, u32[]{:S(2)}) collective-permute-start(bf16[1,64,256]{2,1,0:T(8,128)(2,1)} %get-tuple-element.324), channel_id=1, source_target_pairs={{0,1},{1,2},{2,3},{4,5},{5,6},{6,7},{8,9},{9,10},{10,11},{12,13},{... | collective-permute-start | bytes 98312 | tf_op jit(solution)/shard_map/ppermute | solution.py:35
  108.6 7.4 collective-permute-start.11
  113.2 3.9 collective-permute-start.3
  113.3 3.8 collective-permute-start.2
  355.4 124.9 %all-to-all-start.1 = ((bf16[64,64,256]{2,1,0:T(8,128)(2,1)}), bf16[64,64,256]{2,1,0:T(8,128)(2,1)}, u32[]{:S(2)}, u32[]{:S(2)}) async-start(bf16[64,64,256]{2,1,0:T(8,128)(2,1)} %stack.7), calls=%async_computation.1 | async-start | bytes 4194304 | tf_op jit(solution)/shard_map/all_to_all | solution.py:13
  368.1 345.1 %all-gather.7.cloned.1.call-start = ((), (), s32[]{:S(2)}) async-start(), calls=%async_computation.3 | async-start | bytes 2129920 | tf_op jit(solution)/shard_map/all_gather | solution.py:58
  405.0 3.4 collective-permute-start.12
  407.4 3.8 collective-permute-start.13
  415.1 628.4 %all-reduce.5.cloned.1.call-start = ((), (), s32[]{:S(2)}) async-start(), calls=%async_computation.4 | async-start | bytes 9437184 | tf_op jit(solution)/shard_map/psum | solution.py:154
  415.1 67.8 %collective-permute-start.5 = (bf16[1,64,256]{2,1,0:T(8,128)(2,1)}, bf16[1,64,256]{2,1,0:T(8,128)(2,1)S(1)}, u32[]{:S(2)}, u32[]{:S(2)}) collective-permute-start(bf16[1,64,256]{2,1,0:T(8,128)(2,1)} %get-tuple-element.342), channel_id=1, source_target_pairs={{1,0},{2,1},{3,2},{5,4},{6,5},{7,6},{9,8},{10,9},{11,10},{13,12},{... | collective-permute-start | bytes 98312 | tf_op jit(solution)/shard_map/ppermute | solution.py:37
  475.8 7.2 collective-permute-start.4
  483.1 8.1 collective-permute-start.7
  483.4 7.8 collective-permute-start.6
  506.5 7.3 collective-permute-start.15
  508.6 6.2 collective-permute-start.14
  (30 other events, 1341.0 us)
Sparse Core Ops, SparseCore 0:
  92.4 248.6 all-gather.4
  415.2 297.9 all-gather.6
  719.3 324.1 all-reduce.4
